TPU v7x, 128 devices: a whole 4x4x4 slice. The times are simulated.
128 devices in a mesh: tm: 2 (over core), rows: 64 (over z, x, y).
Axes of the slice: x: 4, y: 4, z: 4, core: 2. Of those that a mesh axis runs over, the one named last changes fastest.
Arguments:
- feat: bfloat16 [4, 128, 240, 512], P('tm', 'rows'), may hold values from -24 to 24
- norm1_gain: float32 [512], replicated, may hold values from 0.5 to 1.5
- norm1_bias: float32 [512], replicated, may hold values from -3 to 3
- conv_weight: bfloat16 [3, 3, 3, 512, 512], replicated, may hold values from -0.0546875 to 0.0546875
- conv_bias: float32 [512], replicated, may hold values from -3 to 3
- norm2_gain: float32 [512], replicated, may hold values from 0.5 to 1.5
- norm2_bias: float32 [512], replicated, may hold values from -3 to 3
- w_query: bfloat16 [512, 512], replicated, may hold values from -0.44194174 to 0.44194174
- w_key: bfloat16 [512, 512], replicated, may hold values from -1.5467961 to 1.5467961
- w_value: bfloat16 [512, 512], replicated, may hold values from -0.25 to 0.25
- w_out: bfloat16 [512, 512], replicated, may hold values from -0.25 to 0.25
- out_bias: float32 [512], replicated, may hold values from -3 to 3
Outputs:
- block_out: bfloat16 [4, 128, 240, 512], P('tm', 'rows')
All inputs are finite; a program needn't handle non-finite values.
Results may differ from a plain program's by a relative error of at most 0.0062.
The roundings to bfloat16 on the way count: a program that leaves them out, or rounds other values in their place, can miss the bound.
Values may be sent and summed in bfloat16 or wider, within the bound.
No kernel may reach another device: no remote copies, remote signals or barrier semaphores. Data moves between devices by JAX's collectives and lax.ppermute only.
A program may use at most 128 MiB of HBM per device.

v0:
```python
import math
import jax
import jax.numpy as jnp
from jax import lax
from jax.sharding import PartitionSpec as P

GROUPS = 32
RADIUS = 4
EPS = 1e-06


def from_behind(array, axis, by):
    peers = lax.axis_size(axis)
    pairs = [(i, i + by) for i in range(peers) if 0 <= i + by < peers]
    return lax.ppermute(array, axis, pairs)


def padded_2(cells, sides, width):
    for axis, dim in sides:
        count = lax.axis_size(axis)
        ends = count - 1
        head = lax.slice_in_dim(cells, 0, width, axis=dim)
        tail = lax.slice_in_dim(cells, cells.shape[dim] - width, cells.shape[dim], axis=dim)
        cells = jnp.concatenate(
            [
                lax.ppermute(tail, axis, [(i, (i + 1) % count) for i in range(ends)]),
                cells,
                lax.ppermute(head, axis, [((i + 1) % count, i) for i in range(ends)]),
            ],
            axis=dim,
        )
    return cells


def group_norm(values, gain, shift, count):
    chans = values.shape[-1]
    grouped = values.reshape(values.shape[:-1] + (GROUPS, chans // GROUPS))
    local_sum = jnp.sum(grouped, axis=(0, 1, 2, 4))
    mean = lax.psum(local_sum, ("tm", "rows")) / count
    centered = grouped - mean[:, None]
    spread = lax.psum(jnp.sum(centered * centered, axis=(0, 1, 2, 4)), ("tm", "rows")) / count
    normed = centered * lax.rsqrt(spread + EPS)[:, None]
    return normed.reshape(values.shape) * gain + shift


def conv_taps(padded, weight, frames, height, width):
    chans = padded.shape[-1]
    total = jnp.zeros((frames * height * width, weight.shape[-1]), jnp.float32)
    for step_t in range(3):
        for step_h in range(3):
            slab = padded[step_t : step_t + frames, step_h : step_h + height]
            stacked = jnp.concatenate(
                [slab[:, :, step_w : step_w + width] for step_w in range(3)], axis=-1
            )
            total = total + jnp.dot(
                stacked.reshape(-1, 3 * chans),
                weight[step_t, step_h].reshape(3 * chans, -1),
                preferred_element_type=jnp.float32,
            )
    return total.reshape(frames, height, width, -1)


def project(flat, weight):
    return jnp.dot(flat, weight, preferred_element_type=jnp.float32).astype(jnp.bfloat16)


def shards(
    feat,
    norm1_gain,
    norm1_bias,
    conv_weight,
    conv_bias,
    norm2_gain,
    norm2_bias,
    w_query,
    w_key,
    w_value,
    w_out,
    out_bias,
):
    frames, stripe_rows, width, chans = feat.shape
    stripes = lax.axis_size("rows")
    count = lax.axis_size("tm") * stripes * frames * stripe_rows * width * (chans // GROUPS)
    act = jax.nn.silu(group_norm(feat.astype(jnp.float32), norm1_gain, norm1_bias, count)).astype(
        jnp.bfloat16
    )
    earlier = from_behind(act, "tm", 1)
    opening = jnp.broadcast_to(act[:1], earlier.shape)
    earlier = jnp.where(lax.axis_index("tm") == 0, opening, earlier)
    timed = jnp.concatenate([earlier, act], axis=0)
    rimmed = padded_2(timed, (("rows", 1),), 1)
    padded = jnp.pad(rimmed, ((0, 0), (0, 0), (1, 1), (0, 0)))
    conv = conv_taps(padded, conv_weight, frames, stripe_rows, width) + conv_bias
    resid = (feat.astype(jnp.float32) + conv).astype(jnp.bfloat16)
    normed = group_norm(resid.astype(jnp.float32), norm2_gain, norm2_bias, count).astype(
        jnp.bfloat16
    )
    flat = normed.reshape(-1, chans)
    query = project(flat, w_query).reshape(frames, -1, chans)
    reach = RADIUS * stripe_rows
    paired = jnp.stack([project(flat, w_key), project(flat, w_value)]).reshape(
        2, frames, stripe_rows, width, chans
    )
    pieces = []
    for offset in range(-RADIUS, RADIUS + 1):
        if offset == 0:
            pieces.append(paired)
        else:
            pieces.append(from_behind(paired, "rows", -offset))
    wide = jnp.concatenate(pieces, axis=2)
    keys = wide[0].reshape(frames, -1, chans)
    values = wide[1].reshape(frames, -1, chans)
    span = 2 * reach + stripe_rows
    place = lax.axis_index("rows") * stripe_rows - reach + jnp.arange(span, dtype=jnp.int32)
    valid = jnp.repeat((place >= 0) & (place < stripes * stripe_rows), width)
    scale = 1.0 / math.sqrt(chans)
    scores = jnp.einsum("fqc,fkc->fqk", query, keys, preferred_element_type=jnp.float32) * scale
    scores = jnp.where(valid[None, None, :], scores, jnp.float32(-1e30))
    top = jnp.max(scores, axis=-1, keepdims=True)
    expo = jnp.exp(scores - top)
    total = jnp.sum(expo, axis=-1, keepdims=True)
    mixed = jnp.einsum(
        "fqk,fkc->fqc", expo.astype(jnp.bfloat16), values, preferred_element_type=jnp.float32
    )
    attn = (mixed / total).astype(jnp.bfloat16).reshape(-1, chans)
    output = jnp.dot(attn, w_out, preferred_element_type=jnp.float32).reshape(
        frames, stripe_rows, width, chans
    )
    return (resid.astype(jnp.float32) + out_bias + output).astype(jnp.bfloat16)


def solution(mesh):
    return jax.shard_map(
        shards,
        mesh=mesh,
        in_specs=(
            P("tm", "rows", None, None),
            P(),
            P(),
            P(),
            P(),
            P(),
            P(),
            P(),
            P(),
            P(),
            P(),
            P(),
        ),
        out_specs=P("tm", "rows", None, None),
        check_vma=False,
    )
```

profile of v0, /device:TPU:54, one launch (start us, length us, event | category | flops | bytes accessed | tf_op | source)
XLA Modules:
  0.0 680.6 jit_solution(8682278299150185639)
XLA Ops:
  0.0 1.5 convert_reduce_fusion.1
  1.7 63.7 %psum.28 = f32[32]{0:T(128)S(1)} all-reduce(f32[32]{0:T(128)S(1)} %reduce_sum.59), channel_id=1, replica_groups=mesh['tm'=2,'rows'=64] {'tm','rows'}, use_global_device_ids=true, to_apply=%region_2.0 | all-reduce | flops 32 | bytes 256 | tf_op jit(solution)/shard_map/psum | solution.py:39
  65.5 1.5 fusion.23
  67.2 63.0 %psum.29 = f32[32]{0:T(128)S(1)} all-reduce(f32[32]{0:T(128)S(1)} %reduce_sum.62), channel_id=1, replica_groups=mesh['tm'=2,'rows'=64] {'tm','rows'}, use_global_device_ids=true, to_apply=%region_5.6 | all-reduce | flops 32 | bytes 256 | tf_op jit(solution)/shard_map/psum | solution.py:41
  130.4 1.9 fusion.31
  132.3 1.7 collective-permute-start
  134.1 2.1 collective-permute-done
  136.5 3.7 collective-permute-start.1
  140.2 2.4 collective-permute-start.2
  142.5 9.3 %fusion.44 = (bf16[1,1,3,512,512]{4,3,2,1,0:T(8,128)(2,1)S(1)}, bf16[1,1,3,512,512]{4,3,2,1,0:T(8,128)(2,1)}, bf16[1,1,3,512,512]{4,3,2,1,0:T(8,128)(2,1)}, bf16...) fusion(bf16[3,3,3,512,512]{4,3,2,1,0:T(8,128)(2,1)} %param.15), kind=kLoop, calls=%fused_computation.89 | loop fusion | bytes 28311552 | tf_op jit(solution)/shard_map/slice | solution.py:57
  151.8 10.6 %collective-permute-done.1 = bf16[4,1,240,512]{3,2,1,0:T(8,128)(2,1)S(1)} collective-permute-done((bf16[4,1,240,512]{3,2,1,0:T(8,128)(2,1)S(1)}, bf16[4,1,240,512]{3,2,1,0:T(8,128)(2,1)S(1)}, u32[]{:S(2)}, u32[]{:S(2)}) %collective-permute-start.1) | collective-permute-done | bytes 983072 | tf_op jit(solution)/shard_map/ppermute | solution.py:26
  162.4 4.4 collective-permute-done.2
  166.8 2.1 select_maximum_fusion
  168.8 6.3 fusion.45
  175.1 0.6 pad_maximum_fusion.3
  176.3 0.9 copy-done.10
  178.5 1.0 copy-done.21
  179.5 1.7 fusion.48
  181.2 1.7 fusion.50
  183.3 0.5 pad_maximum_fusion.5
  183.8 0.9 copy-done.19
  184.7 1.7 fusion.51
  186.4 1.7 fusion.53
  188.1 0.4 pad_maximum_fusion.7
  188.5 1.0 copy-done.17
  189.5 1.7 fusion.54
  191.2 0.9 pad_maximum_fusion.2
  192.1 0.5 copy-done.16
  192.6 1.7 fusion.49
  194.3 1.7 fusion.52
  196.0 1.7 fusion.55
  197.7 2.5 add_add_fusion
  200.2 0.4 convert_reduce_fusion
  200.8 66.5 %psum.30 = f32[32]{0:T(128)S(1)} all-reduce(f32[32]{0:T(128)S(1)} %reduce_sum.81), channel_id=1, replica_groups=mesh['tm'=2,'rows'=64] {'tm','rows'}, use_global_device_ids=true, to_apply=%region_8.9 | all-reduce | flops 32 | bytes 256 | tf_op jit(solution)/shard_map/psum | solution.py:39
  268.0 64.1 %psum.31 = f32[32]{0:T(128)S(1)} all-reduce(f32[32]{0:T(128)S(1)} %reduce_sum.84), channel_id=1, replica_groups=mesh['tm'=2,'rows'=64] {'tm','rows'}, use_global_device_ids=true, to_apply=%region_11.12 | all-reduce | flops 32 | bytes 256 | tf_op jit(solution)/shard_map/psum | solution.py:41
  332.7 0.7 convolution_convert_fusion.1
  333.4 1.7 convolution_convert_fusion
  335.1 1.5 pad_maximum_fusion.10
  336.6 3.8 collective-permute-start.3
  340.4 3.2 collective-permute-start.4
  343.6 4.6 collective-permute-start.5
  348.2 3.0 collective-permute-start.6
  351.2 2.8 collective-permute-start.7
  354.1 30.5 %collective-permute-done.3 = bf16[2,2,2,240,512]{4,3,2,1,0:T(8,128)(2,1)} collective-permute-done((bf16[2,2,2,240,512]{4,3,2,1,0:T(8,128)(2,1)}, bf16[2,2,2,240,512]{4,3,2,1,0:T(8,128)(2,1)}, u32[]{:S(2)}, u32[]{:S(2)}) %collective-permute-start.3) | collective-permute-done | bytes 1966112 | tf_op jit(solution)/shard_map/ppermute | solution.py:15
  384.6 2.5 collective-permute-start.8
  387.1 39.4 %collective-permute-done.4 = bf16[2,2,2,240,512]{4,3,2,1,0:T(8,128)(2,1)} collective-permute-done((bf16[2,2,2,240,512]{4,3,2,1,0:T(8,128)(2,1)}, bf16[2,2,2,240,512]{4,3,2,1,0:T(8,128)(2,1)}, u32[]{:S(2)}, u32[]{:S(2)}) %collective-permute-start.4) | collective-permute-done | bytes 1966112 | tf_op jit(solution)/shard_map/ppermute | solution.py:15
  426.5 90.0 %collective-permute-start.9 = (bf16[2,2,2,240,512]{4,3,2,1,0:T(8,128)(2,1)}, bf16[2,2,2,240,512]{4,3,2,1,0:T(8,128)(2,1)}, u32[]{:S(2)}, u32[]{:S(2)}) collective-permute-start(bf16[2,2,2,240,512]{4,3,2,1,0:T(8,128)(2,1)} %pad_maximum_fusion.10), channel_id=1, source_target_pairs={{3,0},{4,1},{5,2},{6,3},{7,4},{8,5},{9,6},{10,7},{11,8},{12,9},{13... | collective-permute-start | bytes 5898248 | tf_op jit(solution)/shard_map/ppermute | solution.py:15
  516.5 3.1 collective-permute-start.10
  519.8 2.7 convolution_convert_fusion.2
  522.5 1.7 constant_dynamic-update-slice_fusion.8
  524.2 1.7 constant_dynamic-update-slice_fusion.7
  525.9 1.7 constant_dynamic-update-slice_fusion.6
  527.6 1.7 constant_dynamic-update-slice_fusion.5
  529.4 1.7 constant_dynamic-update-slice_fusion.3
  531.1 1.7 constant_dynamic-update-slice_fusion.2
  532.8 27.3 %collective-permute-done.9 = bf16[2,2,2,240,512]{4,3,2,1,0:T(8,128)(2,1)} collective-permute-done((bf16[2,2,2,240,512]{4,3,2,1,0:T(8,128)(2,1)}, bf16[2,2,2,240,512]{4,3,2,1,0:T(8,128)(2,1)}, u32[]{:S(2)}, u32[]{:S(2)}) %collective-permute-start.9) | collective-permute-done | bytes 1966112 | tf_op jit(solution)/shard_map/ppermute | solution.py:15
  560.0 1.7 constant_dynamic-update-slice_fusion.1
  561.7 80.5 %collective-permute-done.10 = bf16[2,2,2,240,512]{4,3,2,1,0:T(8,128)(2,1)} collective-permute-done((bf16[2,2,2,240,512]{4,3,2,1,0:T(8,128)(2,1)}, bf16[2,2,2,240,512]{4,3,2,1,0:T(8,128)(2,1)}, u32[]{:S(2)}, u32[]{:S(2)}) %collective-permute-start.10) | collective-permute-done | bytes 1966112 | tf_op jit(solution)/shard_map/ppermute | solution.py:15
  642.2 1.7 constant_dynamic-update-slice_fusion
  643.9 4.3 fusion.43
  648.2 10.2 %fusion = (f32[2,480]{1,0:T(2,128)S(1)}, f32[2,480,4320]{2,1,0:T(8,128)}) fusion(pred[4320]{0:T(1024)(128)(4,1)S(1)} %broadcast_in_dim.35, bf16[2,480,512]{2,1,0:T(8,128)(2,1)} %bitcast.89, bf16[2,4320,512]{2,1,0:T(8,128)(2,1)S(1)} %bitcast.63), kind=kOutput, calls=%fused_computation.2 | convolution fusion | flops 4259173376 | bytes 26427360 | tf_op jit(solution)/shard_map/fqc,fkc->fqk/dot_general | solution.py:117
  658.4 9.5 %fusion.1 = f32[2,480]{1,0:T(2,128)S(1)} fusion(f32[2,480,4320]{2,1,0:T(8,128)} %get-tuple-element.50, f32[2,480]{1,0:T(2,128)S(1)} %get-tuple-element.49, pred[4320]{0:T(1024)(128)(4,1)S(1)} %broadcast_in_dim.35), kind=kLoop, calls=%fused_computation.3 | loop fusion | flops 16587840 | bytes 16600800 | tf_op jit(solution)/shard_map/reduce_sum | solution.py:121
  667.9 11.0 %divide_convert_fusion = bf16[2,480,512]{2,1,0:T(8,128)(2,1)S(1)} fusion(bf16[2,4320,512]{2,1,0:T(8,128)(2,1)} %bitcast.62, f32[2,480,4320]{2,1,0:T(8,128)} %get-tuple-element.50, f32[2,480]{1,0:T(2,128)S(1)} %get-tuple-element.49, pred[4320]{0:T(1024)(128)(4,1)S(1)} %broadcast_in_dim.35, f32[2,480]{1,0:T(2,128)S(1)} %fusion.1), kind=kOutput, calls=%fused_computation.62 | convolution fusion | flops 4264304640 | bytes 26431200 | tf_op jit(solution)/shard_map/fqk,fkc->fqc/dot_general | solution.py:122
  679.0 1.6 fusion.34
  (89 shorter events, 5.0 us)
Async XLA Ops:
  0.0 332.7 %copy-start = (bf16[512,512]{1,0:T(8,128)(2,1)S(1)}, bf16[512,512]{1,0:T(8,128)(2,1)}, u32[]{:S(2)}) copy-start(bf16[512,512]{1,0:T(8,128)(2,1)} %param.20) | copy-start | bytes 1572868
  132.3 3.9 collective-permute-start
  136.5 25.9 %collective-permute-start.1 = (bf16[4,1,240,512]{3,2,1,0:T(8,128)(2,1)S(1)}, bf16[4,1,240,512]{3,2,1,0:T(8,128)(2,1)S(1)}, u32[]{:S(2)}, u32[]{:S(2)}) collective-permute-start(bf16[4,1,240,512]{3,2,1,0:T(8,128)(2,1)S(1)} %get-tuple-element.44), channel_id=1, source_target_pairs={{0,1},{1,2},{2,3},{3,4},{4,5},{5,6},{6,7},{7,8},{8,9},{9,10},{10,1... | collective-permute-start | bytes 2949128 | tf_op jit(solution)/shard_map/ppermute | solution.py:26
  140.2 26.6 %collective-permute-start.2 = (bf16[4,1,240,512]{3,2,1,0:T(8,128)(2,1)S(1)}, bf16[4,1,240,512]{3,2,1,0:T(8,128)(2,1)S(1)}, u32[]{:S(2)}, u32[]{:S(2)}) collective-permute-start(bf16[4,1,240,512]{3,2,1,0:T(8,128)(2,1)S(1)} %get-tuple-element.45), channel_id=1, source_target_pairs={{1,0},{2,1},{3,2},{4,3},{5,4},{6,5},{7,6},{8,7},{9,8},{10,9},{11,1... | collective-permute-start | bytes 2949128 | tf_op jit(solution)/shard_map/ppermute | solution.py:28
  176.0 1.2 copy-start.10
  176.0 1.5 copy-start.11
  176.0 1.8 copy-start.12
  176.0 2.1 copy-start.13
  178.1 1.4 copy-start.21
  179.5 1.7 copy-start.20
  181.2 1.7 copy-start.6
  181.2 1.7 copy-start.7
  181.2 1.8 copy-start.8
  181.2 2.1 copy-start.9
  183.3 1.4 copy-start.19
  184.7 1.7 copy-start.18
  186.4 1.7 copy-start.5
  188.1 1.4 copy-start.17
  191.2 1.4 copy-start.16
  192.6 1.7 copy-start.15
  194.3 1.7 copy-start.14
  197.7 2.5 copy-start.2
  197.7 2.5 copy-start.24
  200.2 132.1 %copy-start.25 = (f32[512]{0:T(512)S(1)}, f32[512]{0:T(512)}, u32[]{:S(2)}) copy-start(f32[512]{0:T(512)} %param.18) | copy-start | bytes 6148
  200.2 132.1 %copy-start.26 = (f32[512]{0:T(512)S(1)}, f32[512]{0:T(512)}, u32[]{:S(2)}) copy-start(f32[512]{0:T(512)} %param.17) | copy-start | bytes 6148
  200.6 132.8 %copy-start.3 = (bf16[2,2,240,512]{3,2,1,0:T(8,128)(2,1)}, bf16[2,2,240,512]{3,2,1,0:T(8,128)(2,1)S(1)}, u32[]{:S(2)}) copy-start(bf16[2,2,240,512]{3,2,1,0:T(8,128)(2,1)S(1)} %get-tuple-element.6) | copy-start | bytes 2949124
  332.7 2.4 copy-start.22
  335.1 184.7 %copy-start.23 = (bf16[2,2,240,512]{3,2,1,0:T(8,128)(2,1)S(1)}, bf16[2,2,240,512]{3,2,1,0:T(8,128)(2,1)}, u32[]{:S(2)}) copy-start(bf16[2,2,240,512]{3,2,1,0:T(8,128)(2,1)} %copy-done.22) | copy-start | bytes 2949124
  336.6 48.0 %collective-permute-start.3 = (bf16[2,2,2,240,512]{4,3,2,1,0:T(8,128)(2,1)}, bf16[2,2,2,240,512]{4,3,2,1,0:T(8,128)(2,1)}, u32[]{:S(2)}, u32[]{:S(2)}) collective-permute-start(bf16[2,2,2,240,512]{4,3,2,1,0:T(8,128)(2,1)} %pad_maximum_fusion.10), channel_id=1, source_target_pairs={{0,4},{1,5},{2,6},{3,7},{4,8},{5,9},{6,10},{7,11},{8,12},{9,13},{1... | collective-permute-start | bytes 5898248 | tf_op jit(solution)/shard_map/ppermute | solution.py:15
  340.4 86.0 %collective-permute-start.4 = (bf16[2,2,2,240,512]{4,3,2,1,0:T(8,128)(2,1)}, bf16[2,2,2,240,512]{4,3,2,1,0:T(8,128)(2,1)}, u32[]{:S(2)}, u32[]{:S(2)}) collective-permute-start(bf16[2,2,2,240,512]{4,3,2,1,0:T(8,128)(2,1)} %pad_maximum_fusion.10), channel_id=1, source_target_pairs={{0,3},{1,4},{2,5},{3,6},{4,7},{5,8},{6,9},{7,10},{8,11},{9,12},{10... | collective-permute-start | bytes 5898248 | tf_op jit(solution)/shard_map/ppermute | solution.py:15
  343.6 172.8 %collective-permute-start.5 = (bf16[2,2,2,240,512]{4,3,2,1,0:T(8,128)(2,1)}, bf16[2,2,2,240,512]{4,3,2,1,0:T(8,128)(2,1)}, u32[]{:S(2)}, u32[]{:S(2)}) collective-permute-start(bf16[2,2,2,240,512]{4,3,2,1,0:T(8,128)(2,1)} %pad_maximum_fusion.10), channel_id=1, source_target_pairs={{0,2},{1,3},{2,4},{3,5},{4,6},{5,7},{6,8},{7,9},{8,10},{9,11},{10,... | collective-permute-start | bytes 5898248 | tf_op jit(solution)/shard_map/ppermute | solution.py:15
  348.2 179.4 %collective-permute-start.6 = (bf16[2,2,2,240,512]{4,3,2,1,0:T(8,128)(2,1)}, bf16[2,2,2,240,512]{4,3,2,1,0:T(8,128)(2,1)}, u32[]{:S(2)}, u32[]{:S(2)}) collective-permute-start(bf16[2,2,2,240,512]{4,3,2,1,0:T(8,128)(2,1)} %pad_maximum_fusion.10), channel_id=1, source_target_pairs={{0,1},{1,2},{2,3},{3,4},{4,5},{5,6},{6,7},{7,8},{8,9},{9,10},{10,1... | collective-permute-start | bytes 5898248 | tf_op jit(solution)/shard_map/ppermute | solution.py:15
  351.2 178.2 %collective-permute-start.7 = (bf16[2,2,2,240,512]{4,3,2,1,0:T(8,128)(2,1)}, bf16[2,2,2,240,512]{4,3,2,1,0:T(8,128)(2,1)}, u32[]{:S(2)}, u32[]{:S(2)}) collective-permute-start(bf16[2,2,2,240,512]{4,3,2,1,0:T(8,128)(2,1)} %pad_maximum_fusion.10), channel_id=1, source_target_pairs={{1,0},{2,1},{3,2},{4,3},{5,4},{6,5},{7,6},{8,7},{9,8},{10,9},{11,1... | collective-permute-start | bytes 5898248 | tf_op jit(solution)/shard_map/ppermute | solution.py:15
  384.6 146.5 %collective-permute-start.8 = (bf16[2,2,2,240,512]{4,3,2,1,0:T(8,128)(2,1)}, bf16[2,2,2,240,512]{4,3,2,1,0:T(8,128)(2,1)}, u32[]{:S(2)}, u32[]{:S(2)}) collective-permute-start(bf16[2,2,2,240,512]{4,3,2,1,0:T(8,128)(2,1)} %pad_maximum_fusion.10), channel_id=1, source_target_pairs={{2,0},{3,1},{4,2},{5,3},{6,4},{7,5},{8,6},{9,7},{10,8},{11,9},{12,... | collective-permute-start | bytes 5898248 | tf_op jit(solution)/shard_map/ppermute | solution.py:15
  426.5 133.6 %collective-permute-start.9 = (bf16[2,2,2,240,512]{4,3,2,1,0:T(8,128)(2,1)}, bf16[2,2,2,240,512]{4,3,2,1,0:T(8,128)(2,1)}, u32[]{:S(2)}, u32[]{:S(2)}) collective-permute-start(bf16[2,2,2,240,512]{4,3,2,1,0:T(8,128)(2,1)} %pad_maximum_fusion.10), channel_id=1, source_target_pairs={{3,0},{4,1},{5,2},{6,3},{7,4},{8,5},{9,6},{10,7},{11,8},{12,9},{13... | collective-permute-start | bytes 5898248 | tf_op jit(solution)/shard_map/ppermute | solution.py:15
  516.5 125.7 %collective-permute-start.10 = (bf16[2,2,2,240,512]{4,3,2,1,0:T(8,128)(2,1)}, bf16[2,2,2,240,512]{4,3,2,1,0:T(8,128)(2,1)}, u32[]{:S(2)}, u32[]{:S(2)}) collective-permute-start(bf16[2,2,2,240,512]{4,3,2,1,0:T(8,128)(2,1)} %pad_maximum_fusion.10), channel_id=1, source_target_pairs={{4,0},{5,1},{6,2},{7,3},{8,4},{9,5},{10,6},{11,7},{12,8},{13,9},{1... | collective-permute-start | bytes 5898248 | tf_op jit(solution)/shard_map/ppermute | solution.py:15
  667.9 11.1 %copy-start.4 = (bf16[2,2,240,512]{3,2,1,0:T(8,128)(2,1)S(1)}, bf16[2,2,240,512]{3,2,1,0:T(8,128)(2,1)}, u32[]{:S(2)}) copy-start(bf16[2,2,240,512]{3,2,1,0:T(8,128)(2,1)} %copy-done.3) | copy-start | bytes 2949124
  667.9 11.1 %copy-start.27 = (bf16[512,512]{1,0:T(8,128)(2,1)S(1)}, bf16[512,512]{1,0:T(8,128)(2,1)}, u32[]{:S(2)}) copy-start(bf16[512,512]{1,0:T(8,128)(2,1)} %param.22) | copy-start | bytes 1572868
  667.9 11.1 %copy-start.28 = (f32[512]{0:T(512)S(1)}, f32[512]{0:T(512)}, u32[]{:S(2)}) copy-start(f32[512]{0:T(512)} %param.23) | copy-start | bytes 6148
  667.9 12.7 %copy-start.1 = (bf16[512,512]{1,0:T(8,128)(2,1)S(1)}, bf16[512,512]{1,0:T(8,128)(2,1)}, u32[]{:S(2)}) copy-start(bf16[512,512]{1,0:T(8,128)(2,1)} %param.20) | copy-start | bytes 1572868
where the time goes:
time: 682 us; the launch traced here: 681 us
  blocking collectives  257 us (38%)
  waiting for transfers between devices  195 us (29%)
  starting transfers between devices  121 us (18%)
  matrix products  43.8 us (6%)
  local copies, waits for them, and re-layouts  40.4 us (6%)
  other arithmetic  22.8 us (3%)
    ppermute x9, waiting for transfers between devices, from_behind(): return lax.ppermute(array, axis, pairs)  180 us
    psum x2, blocking collectives, group_norm(): mean = lax.psum(local_sum, ('tm', 'rows')) / count  130 us
    psum x2, blocking collectives, group_norm(): lax.psum(jnp.sum(centered * centered, axis=(0, 1, 2, 4)), ('tm', 'rows'))  127 us
    ppermute x9, starting transfers between devices, from_behind(): return lax.ppermute(array, axis, pairs)  115 us
    unnamed x65, local copies, waits for them, and re-layouts  17.3 us
    dot_general x9, matrix products, conv_taps(): jnp.dot(stacked.reshape(-1, 3 * chans), weight[step_t, step_h].reshape(3...  15.9 us
  transfers between devices with their start and end apart: 11, of which 7 were waited for; matrix products, arithmetic and copies ran while one was open for 4% of the time, Pallas kernels for 0%

commit v1 on v0

--- a/solution.py
+++ b/solution.py
@@ -7,6 +7,11 @@
 GROUPS = 32
 RADIUS = 4
 EPS = 1e-06
+
+
+def by_each_axis(array_2, inner_axis, outer_axis):
+    inner = lax.psum(array_2, inner_axis)
+    return lax.psum(inner, outer_axis)
 
 
 def from_behind(array, axis, by):
@@ -38,7 +43,7 @@
     local_sum = jnp.sum(grouped, axis=(0, 1, 2, 4))
     mean = lax.psum(local_sum, ("tm", "rows")) / count
     centered = grouped - mean[:, None]
-    spread = lax.psum(jnp.sum(centered * centered, axis=(0, 1, 2, 4)), ("tm", "rows")) / count
+    spread = by_each_axis(jnp.sum(centered * centered, axis=(0, 1, 2, 4)), "tm", "rows") / count
     normed = centered * lax.rsqrt(spread + EPS)[:, None]
     return normed.reshape(values.shape) * gain + shift
 

time: 682 us -> 849 us (1.24)
  blocking collectives: 257 us -> 464 us
  starting transfers between devices: 121 us -> 85.5 us
    psum x2 -> x4, blocking collectives: 127 us -> 321 us  [the longest x2 316 us: by_each_axis(): return lax.psum(inner, outer_axis)]
    ppermute x9, starting transfers between devices: 115 us -> 79.2 us  [from_behind(): return lax.ppermute(array, axis, pairs)]
    psum x2, blocking collectives: 130 us -> 142 us  [group_norm(): mean = lax.psum(local_sum, ('tm', 'rows')) / count]
  transfers between devices with their start and end apart: 11 -> 11, of which waited for: 7 -> 8; matrix products, arithmetic and copies ran while one was open for 4% -> 3% of each run, Pallas kernels for 0% -> 0%
where the time goes in v1:
time: 849 us; the launch traced here: 848 us
  blocking collectives  464 us (55%)
  waiting for transfers between devices  191 us (22%)
  starting transfers between devices  85.5 us (10%)
  matrix products  43.9 us (5%)
  local copies, waits for them, and re-layouts  40.4 us (5%)
  other arithmetic  22.8 us (3%)
    psum x2, blocking collectives, by_each_axis(): return lax.psum(inner, outer_axis)  316 us
    ppermute x9, waiting for transfers between devices, from_behind(): return lax.ppermute(array, axis, pairs)  173 us
    psum x2, blocking collectives, group_norm(): mean = lax.psum(local_sum, ('tm', 'rows')) / count  142 us
    ppermute x9, starting transfers between devices, from_behind(): return lax.ppermute(array, axis, pairs)  79.2 us
    unnamed x65, local copies, waits for them, and re-layouts  17.3 us
  transfers between devices with their start and end apart: 11, of which 8 were waited for; matrix products, arithmetic and copies ran while one was open for 3% of the time, Pallas kernels for 0%

profile of v1, /device:TPU:54, one launch (start us, length us, event | category | flops | bytes accessed | tf_op | source)
XLA Modules:
  0.0 848.1 jit_solution(14524751550684099938)
XLA Ops:
  0.0 1.5 convert_reduce_fusion.1
  1.7 63.7 %psum.42 = f32[32]{0:T(128)S(1)} all-reduce(f32[32]{0:T(128)S(1)} %reduce_sum.59), channel_id=1, replica_groups=mesh['tm'=2,'rows'=64] {'tm','rows'}, use_global_device_ids=true, to_apply=%region_2.0 | all-reduce | flops 32 | bytes 256 | tf_op jit(solution)/shard_map/psum | solution.py:44
  65.5 1.5 fusion.23
  67.2 2.5 psum.43
  69.7 150.9 %psum.44 = f32[32]{0:T(128)S(1)} all-reduce(f32[32]{0:T(128)S(1)} %psum.43), channel_id=1, replica_groups=mesh['tm'=2,'rows'=64] {'rows'}, use_global_device_ids=true, to_apply=%region_6.7 | all-reduce | flops 32 | bytes 256 | tf_op jit(solution)/shard_map/psum | solution.py:14
  220.8 1.9 fusion.31
  222.7 1.4 collective-permute-start
  224.1 2.1 collective-permute-done
  226.5 4.2 collective-permute-start.1
  230.7 2.1 collective-permute-start.2
  232.8 9.2 %fusion.44 = (bf16[1,1,3,512,512]{4,3,2,1,0:T(8,128)(2,1)S(1)}, bf16[1,1,3,512,512]{4,3,2,1,0:T(8,128)(2,1)}, bf16[1,1,3,512,512]{4,3,2,1,0:T(8,128)(2,1)}, bf16...) fusion(bf16[3,3,3,512,512]{4,3,2,1,0:T(8,128)(2,1)} %param.15), kind=kLoop, calls=%fused_computation.89 | loop fusion | bytes 28311552 | tf_op jit(solution)/shard_map/slice | solution.py:62
  242.0 10.4 %collective-permute-done.1 = bf16[4,1,240,512]{3,2,1,0:T(8,128)(2,1)S(1)} collective-permute-done((bf16[4,1,240,512]{3,2,1,0:T(8,128)(2,1)S(1)}, bf16[4,1,240,512]{3,2,1,0:T(8,128)(2,1)S(1)}, u32[]{:S(2)}, u32[]{:S(2)}) %collective-permute-start.1) | collective-permute-done | bytes 983072 | tf_op jit(solution)/shard_map/ppermute | solution.py:31
  252.4 8.2 collective-permute-done.2
  260.6 2.1 select_maximum_fusion
  262.7 6.3 fusion.45
  268.9 0.6 pad_maximum_fusion.3
  270.1 0.9 copy-done.10
  272.3 1.0 copy-done.21
  273.3 1.7 fusion.48
  275.1 1.7 fusion.50
  277.6 0.9 copy-done.19
  278.5 1.7 fusion.51
  280.2 1.7 fusion.53
  282.4 1.0 copy-done.17
  283.3 1.7 fusion.54
  285.0 0.9 pad_maximum_fusion.2
  285.9 0.5 copy-done.16
  286.4 1.7 fusion.49
  288.2 1.7 fusion.52
  289.8 1.7 fusion.55
  291.6 2.5 add_add_fusion
  294.7 78.8 %psum.45 = f32[32]{0:T(128)S(1)} all-reduce(f32[32]{0:T(128)S(1)} %reduce_sum.81), channel_id=1, replica_groups=mesh['tm'=2,'rows'=64] {'tm','rows'}, use_global_device_ids=true, to_apply=%region_9.10 | all-reduce | flops 32 | bytes 256 | tf_op jit(solution)/shard_map/psum | solution.py:44
  374.2 2.5 psum.46
  376.6 165.2 %psum.47 = f32[32]{0:T(128)S(1)} all-reduce(f32[32]{0:T(128)S(1)} %psum.46), channel_id=1, replica_groups=mesh['tm'=2,'rows'=64] {'rows'}, use_global_device_ids=true, to_apply=%region_13.14 | all-reduce | flops 32 | bytes 256 | tf_op jit(solution)/shard_map/psum | solution.py:14
  542.4 0.7 convolution_convert_fusion.1
  543.1 1.7 convolution_convert_fusion
  544.8 1.5 pad_maximum_fusion.10
  546.3 2.3 collective-permute-start.3
  548.7 1.9 collective-permute-start.4
  550.6 5.7 collective-permute-start.5
  556.3 1.9 collective-permute-start.6
  558.2 3.9 collective-permute-start.7
  562.2 32.8 %collective-permute-done.3 = bf16[2,2,2,240,512]{4,3,2,1,0:T(8,128)(2,1)} collective-permute-done((bf16[2,2,2,240,512]{4,3,2,1,0:T(8,128)(2,1)}, bf16[2,2,2,240,512]{4,3,2,1,0:T(8,128)(2,1)}, u32[]{:S(2)}, u32[]{:S(2)}) %collective-permute-start.3) | collective-permute-done | bytes 1966112 | tf_op jit(solution)/shard_map/ppermute | solution.py:20
  594.9 1.9 collective-permute-start.8
  596.8 31.3 %collective-permute-done.4 = bf16[2,2,2,240,512]{4,3,2,1,0:T(8,128)(2,1)} collective-permute-done((bf16[2,2,2,240,512]{4,3,2,1,0:T(8,128)(2,1)}, bf16[2,2,2,240,512]{4,3,2,1,0:T(8,128)(2,1)}, u32[]{:S(2)}, u32[]{:S(2)}) %collective-permute-start.4) | collective-permute-done | bytes 1966112 | tf_op jit(solution)/shard_map/ppermute | solution.py:20
  628.1 58.3 %collective-permute-start.9 = (bf16[2,2,2,240,512]{4,3,2,1,0:T(8,128)(2,1)}, bf16[2,2,2,240,512]{4,3,2,1,0:T(8,128)(2,1)}, u32[]{:S(2)}, u32[]{:S(2)}) collective-permute-start(bf16[2,2,2,240,512]{4,3,2,1,0:T(8,128)(2,1)} %pad_maximum_fusion.10), channel_id=1, source_target_pairs={{3,0},{4,1},{5,2},{6,3},{7,4},{8,5},{9,6},{10,7},{11,8},{12,9},{13... | collective-permute-start | bytes 5898248 | tf_op jit(solution)/shard_map/ppermute | solution.py:20
  686.4 1.9 collective-permute-start.10
  688.5 2.8 convolution_convert_fusion.2
  691.3 1.7 constant_dynamic-update-slice_fusion.8
  693.0 1.7 constant_dynamic-update-slice_fusion.7
  694.7 1.7 constant_dynamic-update-slice_fusion.6
  696.4 1.7 constant_dynamic-update-slice_fusion.5
  698.2 1.7 constant_dynamic-update-slice_fusion.3
  699.9 2.9 collective-permute-done.8
  702.7 1.7 constant_dynamic-update-slice_fusion.2
  704.4 25.6 %collective-permute-done.9 = bf16[2,2,2,240,512]{4,3,2,1,0:T(8,128)(2,1)} collective-permute-done((bf16[2,2,2,240,512]{4,3,2,1,0:T(8,128)(2,1)}, bf16[2,2,2,240,512]{4,3,2,1,0:T(8,128)(2,1)}, u32[]{:S(2)}, u32[]{:S(2)}) %collective-permute-start.9) | collective-permute-done | bytes 1966112 | tf_op jit(solution)/shard_map/ppermute | solution.py:20
  730.0 1.7 constant_dynamic-update-slice_fusion.1
  731.6 78.1 %collective-permute-done.10 = bf16[2,2,2,240,512]{4,3,2,1,0:T(8,128)(2,1)} collective-permute-done((bf16[2,2,2,240,512]{4,3,2,1,0:T(8,128)(2,1)}, bf16[2,2,2,240,512]{4,3,2,1,0:T(8,128)(2,1)}, u32[]{:S(2)}, u32[]{:S(2)}) %collective-permute-start.10) | collective-permute-done | bytes 1966112 | tf_op jit(solution)/shard_map/ppermute | solution.py:20
  809.7 1.7 constant_dynamic-update-slice_fusion
  811.4 4.3 fusion.43
  815.7 10.1 %fusion = (f32[2,480]{1,0:T(2,128)S(1)}, f32[2,480,4320]{2,1,0:T(8,128)}) fusion(pred[4320]{0:T(1024)(128)(4,1)S(1)} %broadcast_in_dim.35, bf16[2,480,512]{2,1,0:T(8,128)(2,1)} %bitcast.89, bf16[2,4320,512]{2,1,0:T(8,128)(2,1)S(1)} %bitcast.63), kind=kOutput, calls=%fused_computation.2 | convolution fusion | flops 4259173376 | bytes 26427360 | tf_op jit(solution)/shard_map/fqc,fkc->fqk/dot_general | solution.py:122
  825.9 9.5 %fusion.1 = f32[2,480]{1,0:T(2,128)S(1)} fusion(f32[2,480,4320]{2,1,0:T(8,128)} %get-tuple-element.50, f32[2,480]{1,0:T(2,128)S(1)} %get-tuple-element.49, pred[4320]{0:T(1024)(128)(4,1)S(1)} %broadcast_in_dim.35), kind=kLoop, calls=%fused_computation.3 | loop fusion | flops 16587840 | bytes 16600800 | tf_op jit(solution)/shard_map/reduce_sum | solution.py:126
  835.4 11.1 %divide_convert_fusion = bf16[2,480,512]{2,1,0:T(8,128)(2,1)S(1)} fusion(bf16[2,4320,512]{2,1,0:T(8,128)(2,1)} %bitcast.62, f32[2,480,4320]{2,1,0:T(8,128)} %get-tuple-element.50, f32[2,480]{1,0:T(2,128)S(1)} %get-tuple-element.49, pred[4320]{0:T(1024)(128)(4,1)S(1)} %broadcast_in_dim.35, f32[2,480]{1,0:T(2,128)S(1)} %fusion.1), kind=kOutput, calls=%fused_computation.62 | convolution fusion | flops 4264304640 | bytes 26431200 | tf_op jit(solution)/shard_map/fqk,fkc->fqc/dot_general | solution.py:127
  846.4 1.6 fusion.34
  (91 shorter events, 6.4 us)
Async XLA Ops:
  0.0 542.4 %copy-start = (bf16[512,512]{1,0:T(8,128)(2,1)S(1)}, bf16[512,512]{1,0:T(8,128)(2,1)}, u32[]{:S(2)}) copy-start(bf16[512,512]{1,0:T(8,128)(2,1)} %param.20) | copy-start | bytes 1572868
  222.7 3.5 collective-permute-start
  226.5 25.9 %collective-permute-start.1 = (bf16[4,1,240,512]{3,2,1,0:T(8,128)(2,1)S(1)}, bf16[4,1,240,512]{3,2,1,0:T(8,128)(2,1)S(1)}, u32[]{:S(2)}, u32[]{:S(2)}) collective-permute-start(bf16[4,1,240,512]{3,2,1,0:T(8,128)(2,1)S(1)} %get-tuple-element.44), channel_id=1, source_target_pairs={{0,1},{1,2},{2,3},{3,4},{4,5},{5,6},{6,7},{7,8},{8,9},{9,10},{10,1... | collective-permute-start | bytes 2949128 | tf_op jit(solution)/shard_map/ppermute | solution.py:31
  230.7 29.9 %collective-permute-start.2 = (bf16[4,1,240,512]{3,2,1,0:T(8,128)(2,1)S(1)}, bf16[4,1,240,512]{3,2,1,0:T(8,128)(2,1)S(1)}, u32[]{:S(2)}, u32[]{:S(2)}) collective-permute-start(bf16[4,1,240,512]{3,2,1,0:T(8,128)(2,1)S(1)} %get-tuple-element.45), channel_id=1, source_target_pairs={{1,0},{2,1},{3,2},{4,3},{5,4},{6,5},{7,6},{8,7},{9,8},{10,9},{11,1... | collective-permute-start | bytes 2949128 | tf_op jit(solution)/shard_map/ppermute | solution.py:33
  269.8 1.2 copy-start.10
  269.8 1.5 copy-start.11
  269.8 1.8 copy-start.12
  269.9 2.1 copy-start.13
  271.9 1.4 copy-start.21
  273.3 1.7 copy-start.20
  275.0 1.7 copy-start.6
  275.0 1.7 copy-start.7
  275.0 1.8 copy-start.8
  275.1 2.1 copy-start.9
  277.1 1.4 copy-start.19
  278.5 1.7 copy-start.18
  280.2 1.7 copy-start.5
  281.9 1.4 copy-start.17
  285.0 1.4 copy-start.16
  286.4 1.7 copy-start.15
  288.1 1.7 copy-start.14
  291.5 2.5 copy-start.2
  291.5 2.5 copy-start.24
  294.0 248.0 %copy-start.25 = (f32[512]{0:T(512)S(1)}, f32[512]{0:T(512)}, u32[]{:S(2)}) copy-start(f32[512]{0:T(512)} %param.18) | copy-start | bytes 6148
  294.0 248.0 %copy-start.26 = (f32[512]{0:T(512)S(1)}, f32[512]{0:T(512)}, u32[]{:S(2)}) copy-start(f32[512]{0:T(512)} %param.17) | copy-start | bytes 6148
  294.5 248.6 %copy-start.3 = (bf16[2,2,240,512]{3,2,1,0:T(8,128)(2,1)}, bf16[2,2,240,512]{3,2,1,0:T(8,128)(2,1)S(1)}, u32[]{:S(2)}) copy-start(bf16[2,2,240,512]{3,2,1,0:T(8,128)(2,1)S(1)} %get-tuple-element.6) | copy-start | bytes 2949124
  542.4 2.4 copy-start.22
  544.8 143.7 %copy-start.23 = (bf16[2,2,240,512]{3,2,1,0:T(8,128)(2,1)S(1)}, bf16[2,2,240,512]{3,2,1,0:T(8,128)(2,1)}, u32[]{:S(2)}) copy-start(bf16[2,2,240,512]{3,2,1,0:T(8,128)(2,1)} %copy-done.22) | copy-start | bytes 2949124
  546.3 48.6 %collective-permute-start.3 = (bf16[2,2,2,240,512]{4,3,2,1,0:T(8,128)(2,1)}, bf16[2,2,2,240,512]{4,3,2,1,0:T(8,128)(2,1)}, u32[]{:S(2)}, u32[]{:S(2)}) collective-permute-start(bf16[2,2,2,240,512]{4,3,2,1,0:T(8,128)(2,1)} %pad_maximum_fusion.10), channel_id=1, source_target_pairs={{0,4},{1,5},{2,6},{3,7},{4,8},{5,9},{6,10},{7,11},{8,12},{9,13},{1... | collective-permute-start | bytes 5898248 | tf_op jit(solution)/shard_map/ppermute | solution.py:20
  548.7 79.5 %collective-permute-start.4 = (bf16[2,2,2,240,512]{4,3,2,1,0:T(8,128)(2,1)}, bf16[2,2,2,240,512]{4,3,2,1,0:T(8,128)(2,1)}, u32[]{:S(2)}, u32[]{:S(2)}) collective-permute-start(bf16[2,2,2,240,512]{4,3,2,1,0:T(8,128)(2,1)} %pad_maximum_fusion.10), channel_id=1, source_target_pairs={{0,3},{1,4},{2,5},{3,6},{4,7},{5,8},{6,9},{7,10},{8,11},{9,12},{10... | collective-permute-start | bytes 5898248 | tf_op jit(solution)/shard_map/ppermute | solution.py:20
  550.6 135.8 %collective-permute-start.5 = (bf16[2,2,2,240,512]{4,3,2,1,0:T(8,128)(2,1)}, bf16[2,2,2,240,512]{4,3,2,1,0:T(8,128)(2,1)}, u32[]{:S(2)}, u32[]{:S(2)}) collective-permute-start(bf16[2,2,2,240,512]{4,3,2,1,0:T(8,128)(2,1)} %pad_maximum_fusion.10), channel_id=1, source_target_pairs={{0,2},{1,3},{2,4},{3,5},{4,6},{5,7},{6,8},{7,9},{8,10},{9,11},{10,... | collective-permute-start | bytes 5898248 | tf_op jit(solution)/shard_map/ppermute | solution.py:20
  556.3 140.1 %collective-permute-start.6 = (bf16[2,2,2,240,512]{4,3,2,1,0:T(8,128)(2,1)}, bf16[2,2,2,240,512]{4,3,2,1,0:T(8,128)(2,1)}, u32[]{:S(2)}, u32[]{:S(2)}) collective-permute-start(bf16[2,2,2,240,512]{4,3,2,1,0:T(8,128)(2,1)} %pad_maximum_fusion.10), channel_id=1, source_target_pairs={{0,1},{1,2},{2,3},{3,4},{4,5},{5,6},{6,7},{7,8},{8,9},{9,10},{10,1... | collective-permute-start | bytes 5898248 | tf_op jit(solution)/shard_map/ppermute | solution.py:20
  558.2 139.9 %collective-permute-start.7 = (bf16[2,2,2,240,512]{4,3,2,1,0:T(8,128)(2,1)}, bf16[2,2,2,240,512]{4,3,2,1,0:T(8,128)(2,1)}, u32[]{:S(2)}, u32[]{:S(2)}) collective-permute-start(bf16[2,2,2,240,512]{4,3,2,1,0:T(8,128)(2,1)} %pad_maximum_fusion.10), channel_id=1, source_target_pairs={{1,0},{2,1},{3,2},{4,3},{5,4},{6,5},{7,6},{8,7},{9,8},{10,9},{11,1... | collective-permute-start | bytes 5898248 | tf_op jit(solution)/shard_map/ppermute | solution.py:20
  594.9 107.8 %collective-permute-start.8 = (bf16[2,2,2,240,512]{4,3,2,1,0:T(8,128)(2,1)}, bf16[2,2,2,240,512]{4,3,2,1,0:T(8,128)(2,1)}, u32[]{:S(2)}, u32[]{:S(2)}) collective-permute-start(bf16[2,2,2,240,512]{4,3,2,1,0:T(8,128)(2,1)} %pad_maximum_fusion.10), channel_id=1, source_target_pairs={{2,0},{3,1},{4,2},{5,3},{6,4},{7,5},{8,6},{9,7},{10,8},{11,9},{12,... | collective-permute-start | bytes 5898248 | tf_op jit(solution)/shard_map/ppermute | solution.py:20
  628.1 101.8 %collective-permute-start.9 = (bf16[2,2,2,240,512]{4,3,2,1,0:T(8,128)(2,1)}, bf16[2,2,2,240,512]{4,3,2,1,0:T(8,128)(2,1)}, u32[]{:S(2)}, u32[]{:S(2)}) collective-permute-start(bf16[2,2,2,240,512]{4,3,2,1,0:T(8,128)(2,1)} %pad_maximum_fusion.10), channel_id=1, source_target_pairs={{3,0},{4,1},{5,2},{6,3},{7,4},{8,5},{9,6},{10,7},{11,8},{12,9},{13... | collective-permute-start | bytes 5898248 | tf_op jit(solution)/shard_map/ppermute | solution.py:20
  686.4 123.3 %collective-permute-start.10 = (bf16[2,2,2,240,512]{4,3,2,1,0:T(8,128)(2,1)}, bf16[2,2,2,240,512]{4,3,2,1,0:T(8,128)(2,1)}, u32[]{:S(2)}, u32[]{:S(2)}) collective-permute-start(bf16[2,2,2,240,512]{4,3,2,1,0:T(8,128)(2,1)} %pad_maximum_fusion.10), channel_id=1, source_target_pairs={{4,0},{5,1},{6,2},{7,3},{8,4},{9,5},{10,6},{11,7},{12,8},{13,9},{1... | collective-permute-start | bytes 5898248 | tf_op jit(solution)/shard_map/ppermute | solution.py:20
  835.3 11.1 %copy-start.4 = (bf16[2,2,240,512]{3,2,1,0:T(8,128)(2,1)S(1)}, bf16[2,2,240,512]{3,2,1,0:T(8,128)(2,1)}, u32[]{:S(2)}) copy-start(bf16[2,2,240,512]{3,2,1,0:T(8,128)(2,1)} %copy-done.3) | copy-start | bytes 2949124
  835.3 11.1 %copy-start.27 = (bf16[512,512]{1,0:T(8,128)(2,1)S(1)}, bf16[512,512]{1,0:T(8,128)(2,1)}, u32[]{:S(2)}) copy-start(bf16[512,512]{1,0:T(8,128)(2,1)} %param.22) | copy-start | bytes 1572868
  835.3 11.1 %copy-start.28 = (f32[512]{0:T(512)S(1)}, f32[512]{0:T(512)}, u32[]{:S(2)}) copy-start(f32[512]{0:T(512)} %param.23) | copy-start | bytes 6148
  835.3 12.7 %copy-start.1 = (bf16[512,512]{1,0:T(8,128)(2,1)S(1)}, bf16[512,512]{1,0:T(8,128)(2,1)}, u32[]{:S(2)}) copy-start(bf16[512,512]{1,0:T(8,128)(2,1)} %param.20) | copy-start | bytes 1572868
